TPU v7x, 32 devices: a whole 2x2x4 slice. The times are simulated.
32 devices in a mesh: arow: 4 (over z), acol: 8 (over y, x, core).
Axes of the slice: x: 2, y: 2, z: 4, core: 2. Of those that a mesh axis runs over, the one named last changes fastest.
Arguments:
- row_data: bfloat16 [65536, 128], P(('arow', 'acol')), may hold values from -96 to 96
- row_baseline: int32 [65536], P(('arow', 'acol')), may hold values from 0 to 131071, as said below
- pair_table: int32 [131072, 2], P(('arow', 'acol')), may hold values from 0 to 2047, as said below
- lengths: int32 [131072], P(('arow', 'acol')), may hold values from 1 to 8
- model_vis: bfloat16 [2048, 2048, 128], P('arow', 'acol'), may hold values from -6 to 6
- gains: float32 [2048, 128], P(('arow', 'acol')), may hold values from -6 to 6
Outputs:
- new_gains: float32 [2048, 128], P(('arow', 'acol'))
Inputs may be any that keep to these rules, and one draw needn't show every extreme that they name: `pair_table`: slot j belongs to tile o = j // 4096; its first antenna lies in 512 * (o // 8) to 512 * (o // 8 + 1) - 1, its second in 256 * (o % 8) to 256 * (o % 8 + 1) - 1, and the two differ. `row_baseline`: the rows of one device name slots of one tile at most 256 times; one tile is named exactly 256 times by the rows of every device.
All inputs are finite; a program needn't handle non-finite values.
Results may differ from a plain program's by a relative error of at most 0.0003.
Values may be sent and summed in bfloat16 or wider, within the bound.
No kernel may reach another device: no remote copies, remote signals or barrier semaphores. Data moves between devices by JAX's collectives and lax.ppermute only.
A program may use at most 128 MiB of HBM per device.

v0:
```python
import math

import jax
import jax.numpy as jnp
from jax import lax
from jax.sharding import PartitionSpec as P

RIDGE = 1.0


def local(row_data, row_baseline, pair_table, lengths, model_vis, gains):
    row_count = lax.axis_size("arow")
    col_count = lax.axis_size("acol")
    devices = row_count * col_count
    count_rows = row_data.shape[0]
    width = row_data.shape[1]
    half = width // 2
    slots = lengths.shape[0]
    capacity = 4 * count_rows // devices
    row_block = model_vis.shape[0]
    col_block = model_vis.shape[1]
    my_row = lax.axis_index("arow")
    my_col = lax.axis_index("acol")
    owner = row_baseline // slots
    local_id = row_baseline - owner * slots
    hits = (owner[:, None] == jnp.arange(devices, dtype=jnp.int32)[None, :]).astype(jnp.bfloat16)
    step_rows = math.gcd(count_rows, 128)
    block_count = count_rows // step_rows
    blocks = hits.reshape(block_count, step_rows, devices)
    positions = jnp.arange(step_rows, dtype=jnp.int32)
    lower = (positions[:, None] > positions[None, :]).astype(jnp.bfloat16)
    within = jnp.einsum("ij,bjd->bid", lower, blocks, preferred_element_type=jnp.float32)
    per_block = jnp.sum(blocks, axis=1, dtype=jnp.float32)
    before = jnp.cumsum(per_block, axis=0) - per_block
    ranking = jnp.sum((within + before[:, None, :]) * blocks.astype(jnp.float32), axis=2).reshape(
        count_rows
    )
    target = owner * capacity + ranking.astype(jnp.int32)
    code = local_id + 1
    codes = jnp.stack([code // 64, code % 64], axis=1).astype(jnp.bfloat16)
    groups = math.gcd(devices, 16)
    span = devices * capacity // groups

    def place(group):
        wanted = group * span + jnp.arange(span, dtype=jnp.int32)
        table = (target[None, :] == wanted[:, None]).astype(jnp.bfloat16)
        placed = jnp.dot(table, row_data, preferred_element_type=jnp.float32).astype(jnp.bfloat16)
        tagged = jnp.dot(table, codes, preferred_element_type=jnp.float32)
        return (placed, tagged)

    outgoing, tags = lax.map(place, jnp.arange(groups, dtype=jnp.int32))
    outgoing = outgoing.reshape(devices * capacity, width)
    labels = (tags[..., 0] * 64.0 + tags[..., 1]).astype(jnp.int32).reshape(devices * capacity) - 1
    arrived, names = (
        lax.all_to_all(
            outgoing.reshape(devices, capacity, width),
            ("arow", "acol"),
            split_axis=0,
            concat_axis=0,
            tiled=True,
        ),
        lax.all_to_all(
            labels.reshape(devices, capacity),
            ("arow", "acol"),
            split_axis=0,
            concat_axis=0,
            tiled=True,
        ),
    )
    arrived = arrived.reshape(devices * capacity, width)
    names = names.reshape(devices * capacity)
    valid = names >= 0
    safe = jnp.clip(names, 0, slots - 1)
    slot_info = jnp.concatenate([pair_table, lengths[:, None]], axis=1)
    found = jnp.take(slot_info, safe, axis=0)
    first = jnp.clip(found[:, 0] - my_row * row_block, 0, row_block - 1)
    second = jnp.clip(found[:, 1] - my_col * col_block, 0, col_block - 1)
    weight = jnp.where(valid, found[:, 2], 0).astype(jnp.float32)
    every = lax.all_gather(gains, ("arow", "acol"), axis=0, tiled=True)
    column_gains = lax.dynamic_slice_in_dim(every, my_col * col_block, col_block, 0)
    pick_col = (second[:, None] == jnp.arange(col_block, dtype=jnp.int32)[None, :]).astype(
        jnp.float32
    )
    row_gain = jnp.dot(
        pick_col, column_gains, precision=lax.Precision.HIGHEST, preferred_element_type=jnp.float32
    )
    model_rows = jnp.take(
        model_vis.reshape(row_block * col_block, width), first * col_block + second, axis=0
    )
    m_re = model_rows[:, :half].astype(jnp.float32)
    m_im = model_rows[:, half:].astype(jnp.float32)
    g_re = row_gain[:, :half]
    g_im = row_gain[:, half:]
    c_re = m_re * g_re + m_im * g_im
    c_im = m_re * g_im - m_im * g_re
    r_re = arrived[:, :half].astype(jnp.float32) * weight[:, None]
    r_im = arrived[:, half:].astype(jnp.float32) * weight[:, None]
    values = jnp.concatenate(
        [
            c_re * r_re - c_im * r_im,
            c_re * r_im + c_im * r_re,
            weight[:, None] * (c_re * c_re + c_im * c_im),
        ],
        axis=1,
    )
    pick_row = (first[None, :] == jnp.arange(row_block, dtype=jnp.int32)[:, None]).astype(
        jnp.float32
    )
    totals = jnp.dot(
        pick_row, values, precision=lax.Precision.HIGHEST, preferred_element_type=jnp.float32
    )
    numer = totals[:, :width]
    denom = totals[:, width:]
    numer, denom = lax.psum((numer, denom), "acol")
    share = row_block // col_count
    numer = lax.dynamic_slice_in_dim(numer, my_col * share, share, 0)
    denom = lax.dynamic_slice_in_dim(denom, my_col * share, share, 0)
    return jnp.concatenate(
        [numer[:, :half] / (denom + RIDGE), numer[:, half:] / (denom + RIDGE)], axis=1
    )


def solution(mesh):
    placed = (
        P(("arow", "acol"), None),
        P(("arow", "acol")),
        P(("arow", "acol"), None),
        P(("arow", "acol")),
        P("arow", "acol", None),
        P(("arow", "acol"), None),
    )
    return jax.shard_map(
        local, mesh=mesh, in_specs=placed, out_specs=P(("arow", "acol"), None), check_vma=False
    )
```

profile of v0, /device:TPU:0, one launch (start us, length us, event | category | flops | bytes accessed | tf_op | source)
XLA Modules:
  0.0 533.4 jit_solution(483655217040452650)
XLA Ops:
  6.5 0.7 fusion.50
  7.7 0.7 bitcast_add_fusion
  8.5 71.8 %while.12 = (s32[]{:T(128)}, bf16[16,512,128]{2,1,0:T(8,128)(2,1)}, f32[16,512,2]{1,2,0:T(2,128)S(1)}, s32[2048]{0:T(1024)S(1)}, s32[16]{0:T(128)S(1)}, /*index=...) while((s32[]{:T(128)}, bf16[16,512,128]{2,1,0:T(8,128)(2,1)}, ...), condition=%wide.region_4.5_spmd, body=%wide.region_3.4_spmd.sunk | while | flops 274792960 | bytes 690813 | solution.py:51
  9.7 2.4 fusion.73
  12.2 0.8 fusion.74
  14.2 2.5 fusion.73
  16.7 0.8 fusion.74
  18.7 2.5 fusion.73
  21.1 0.8 fusion.74
  23.2 2.5 fusion.73
  25.6 0.8 fusion.74
  27.7 2.5 fusion.73
  30.1 0.8 fusion.74
  32.2 2.4 fusion.73
  34.6 0.8 fusion.74
  36.6 2.5 fusion.73
  39.1 0.8 fusion.74
  41.1 2.5 fusion.73
  43.6 0.8 fusion.74
  45.6 2.5 fusion.73
  48.1 0.8 fusion.74
  50.1 2.5 fusion.73
  52.6 0.8 fusion.74
  54.6 2.5 fusion.73
  57.0 0.8 fusion.74
  59.1 2.5 fusion.73
  61.5 0.8 fusion.74
  63.6 2.5 fusion.73
  66.0 0.8 fusion.74
  68.0 2.5 fusion.73
  70.5 0.8 fusion.74
  72.5 2.5 fusion.73
  75.0 0.8 fusion.74
  77.0 2.5 fusion.73
  79.5 0.8 fusion.74
  80.3 0.7 convert_add_fusion
  81.0 7.3 %all-to-all-start = ((s32[32,1,256]{2,1,0:T(1,128)}), s32[32,1,256]{2,1,0:T(1,128)S(1)}, u32[]{:S(2)}, u32[]{:S(2)}) async-start(s32[32,1,256]{2,1,0:T(1,128)} %bitcast.7), calls=%async_computation | async-start | bytes 65536 | tf_op jit(solution)/shard_map/all_to_all | solution.py:62
  88.3 0.7 all-gather.2.cloned.1.call-update
  89.1 0.6 copy.31
  89.7 4.1 copy.33
  93.8 1.7 all-to-all-done
  95.5 4.3 all-to-all-start.1
  100.1 2.6 copy.28
  102.7 3.3 fusion.31
  106.1 1.7 copy.35
  107.9 27.7 %gather_fusion = s32[8192,3]{1,0:T(8,128)} fusion(s32[4096,3]{1,0:T(8,128)S(1)} %copy.31, s32[8192]{0:T(1024)S(1)} %broadcast_clamp_fusion.1), kind=kCustom, calls=%fused_computation | custom fusion | bytes 229376 | tf_op jit(solution)/shard_map/jit(_take)/gather | solution.py:75
  135.6 6.2 %broadcast_select_fusion = s32[8192,3]{1,0:T(8,128)S(1)} fusion(s32[8192,3]{1,0:T(8,128)} %gather_fusion, pred[8192]{0:T(1024)(128)(4,1)S(1)} %compare_and_fusion), kind=kLoop, calls=%fused_computation.51 | loop fusion | flops 24576 | bytes 204800 | tf_op jit(solution)/shard_map/jit(_take)/select_n | solution.py:75
  141.8 2.2 fusion.33
  144.1 4.9 fusion.58
  149.0 3.2 and_reduce_fusion
  152.2 286.6 %gather_fusion.1 = bf16[8192,128]{1,0:T(8,128)(2,1)S(1)} fusion(bf16[131072,128]{1,0:T(8,128)(2,1)} %bitcast.45, s32[8192]{0:T(1024)S(1)} %broadcast_clamp_fusion), kind=kCustom, calls=%fused_computation.1 | custom fusion | bytes 4227072 | tf_op jit(solution)/shard_map/jit(_take)/gather | solution.py:87
  438.8 3.0 copy.32
  441.7 1.8 broadcast_select_fusion.1
  443.6 7.3 %fusion.25 = f32[8192,128]{0,1:T(8,128)} fusion(s32[8192]{0:T(1024)S(1)} %get-tuple-element.47, f32[2048,128]{1,0:T(8,128)} %all-gather.2.cloned.1.call-done, s32[]{:T(128)S(6)} %select_n.65), kind=kOutput, calls=%fused_computation.22 | convolution fusion | flops 3223322624 | bytes 4358148 | tf_op jit(solution)/shard_map/dot_general | solution.py:84
  450.9 1.9 copy.37
  452.8 0.9 copy-done
  453.7 1.1 multiply_subtract_fusion
  454.8 0.8 multiply_add_fusion
  455.6 9.6 %fusion.23 = f32[512,192]{0,1:T(8,128)S(1)} fusion(s32[8192]{0:T(1024)S(1)} %get-tuple-element.46, f32[8192,64]{0,1:T(8,128)S(1)} %get-tuple-element.68, f32[8192,64]{0,1:T(8,128)S(1)} %get-tuple-element.67, f32[8192,64]{0,1:T(8,128)S(1)} %get-tuple-element.64), kind=kOutput, calls=%fused_computation.17 | convolution fusion | flops 9671016448 | bytes 6717440 | tf_op jit(solution)/shard_map/dot_general | solution.py:109
  465.2 0.7 slice.73
  465.9 0.6 slice.74
  466.6 58.4 %all-reduce.3.cloned.1.call-done = (f32[512,128]{0,1:T(8,128)}, f32[512,64]{0,1:T(8,128)}) async-done(((f32[512,128]{0,1:T(8,128)}, f32[512,64]{0,1:T(8,128)}), (f32[512,128]{0,1:T(8,128)}, f32[512,64]{0,1:T(8,128)})) %all-reduce.3.cloned.1.call-update) | async-done | bytes 393232 | tf_op jit(solution)/shard_map/psum | solution.py:114
  525.0 0.9 dynamic-slice_divide_fusion.1
  525.9 0.7 copy.36
  (59 shorter events, 10.5 us)
Async XLA Ops:
  8.5 80.6 %copy-start.1 = (s32[4096,2]{0,1:T(2,128)S(1)}, s32[4096,2]{0,1:T(2,128)}, u32[]{:S(2)}) copy-start(s32[4096,2]{0,1:T(2,128)} %param.10) | copy-start | bytes 98308
  8.5 80.6 %copy-start.2 = (s32[4096]{0:T(1024)S(1)}, s32[4096]{0:T(1024)}, u32[]{:S(2)}) copy-start(s32[4096]{0:T(1024)} %param.11) | copy-start | bytes 49156
  81.0 14.6 %all-to-all-start = ((s32[32,1,256]{2,1,0:T(1,128)}), s32[32,1,256]{2,1,0:T(1,128)S(1)}, u32[]{:S(2)}, u32[]{:S(2)}) async-start(s32[32,1,256]{2,1,0:T(1,128)} %bitcast.7), calls=%async_computation | async-start | bytes 65536 | tf_op jit(solution)/shard_map/all_to_all | solution.py:62
  88.3 355.3 %all-gather.2.cloned.1.call-start = ((), (), s32[]{:S(2)}) async-start(), calls=%async_computation.2 | async-start | bytes 1081344 | tf_op jit(solution)/shard_map/all_gather | solution.py:79
  95.5 355.4 %all-to-all-start.1 = ((bf16[32,256,128]{1,2,0:T(8,128)(2,1)}), bf16[32,256,128]{1,2,0:T(8,128)(2,1)}, u32[]{:S(2)}, u32[]{:S(2)}) async-start(bf16[32,256,128]{1,2,0:T(8,128)(2,1)} %copy.33), calls=%async_computation.1 | async-start | bytes 4194304 | tf_op jit(solution)/shard_map/all_to_all | solution.py:55
  99.8 425.1 %all-reduce.3.cloned.1.call-start = ((), (), s32[]{:S(2)}) async-start(), calls=%async_computation.3 | async-start | bytes 786432 | tf_op jit(solution)/shard_map/psum | solution.py:114
  450.9 2.8 copy-start
Sparse Core Ops, SparseCore 0:
  92.0 64.4 all-gather.1
  466.7 58.2 all-reduce.2
where the time goes:
time: 536 us; the launch traced here: 533 us
  local copies, waits for them, and re-layouts  341 us (64%)
  matrix products  69.2 us (13%)
  waiting for transfers between devices  60.8 us (11%)
  other arithmetic  27 us (5%)
  between operations  13.7 us (3%)
  starting transfers between devices  11.8 us (2%)
  loops' own time  10.1 us (2%)
    gather x2, local copies, waits for them, and re-layouts, local(): jnp.take(model_vis.reshape(row_block * col_block, width), first * col_blo...  290 us
    psum x1, waiting for transfers between devices, local(): numer, denom = lax.psum((numer, denom), 'acol')  58.4 us
    dot_general x16, matrix products, place(): jnp.dot(table, row_data, preferred_element_type=jnp.float32)  39.3 us
    gather x1, local copies, waits for them, and re-layouts, local(): found = jnp.take(slot_info, safe, axis=0)  27.7 us
    dot_general x16, matrix products, place(): tagged = jnp.dot(table, codes, preferred_element_type=jnp.float32)  12.7 us
  transfers between devices with their start and end apart: 4, of which 2 were waited for; matrix products, arithmetic and copies ran while one was open for 67% of the time, Pallas kernels for 0%

commit v1 on v0

v1 whole, which is shorter than its diff:
```python
import math

import jax
import jax.numpy as jnp
from jax import lax
from jax.experimental import pallas as pl
from jax.experimental.pallas import tpu as pltpu
from jax.sharding import PartitionSpec as P

RIDGE = 1.0
BIG = 60 * 1024 * 1024


def pack_kernel(target, local_id, rows, out, tags, wide, placed):
    count = rows.shape[0]
    wide[...] = rows[...].astype(jnp.float32)
    placed[...] = jnp.zeros(placed.shape, jnp.float32)

    def step(i, carry):
        for j in range(16):
            r = i * 16 + j
            t = target[r]
            tags[t] = local_id[r]
            placed[pl.ds(t, 1), :] = wide[pl.ds(r, 1), :]
        return carry

    lax.fori_loop(0, count // 16, step, 0)
    out[...] = placed[...].astype(jnp.bfloat16)


def model_kernel(key, second, gains, model, out, held, sems):
    chunks = sems.shape[0]
    part = held.shape[0] // chunks
    slots = out.shape[0]

    def copy(i):
        return pltpu.make_async_copy(
            model.at[pl.ds(i * part, part)], held.at[pl.ds(i * part, part)], sems.at[i]
        )

    for i in range(chunks):
        copy(i).start()
    width = out.shape[1]
    sub = lax.broadcasted_iota(jnp.int32, (8, width), 0)

    def gain_step(i, carry):
        acc = jnp.zeros((8, width), jnp.float32)
        for j in range(8):
            q = second[i * 8 + j]
            acc = jnp.where(sub == j, gains[pl.ds(q, 1), :], acc)
        out[pl.ds(pl.multiple_of(i * 8, 8), 8), :] = acc
        return carry

    lax.fori_loop(0, slots // 8, gain_step, 0, unroll=2)
    for i in range(chunks):
        copy(i).wait()
    left = lax.broadcasted_iota(jnp.int32, (8, width), 1) < width // 2

    def step(i, carry):
        m = jnp.zeros((8, width), jnp.float32)
        for j in range(8):
            k = key[i * 8 + j]
            tile = held[k // 8].astype(jnp.float32)
            m = jnp.where(sub == j, pltpu.roll(tile, (j - k) & 7, 0), m)
        at = pl.ds(pl.multiple_of(i * 8, 8), 8)
        g = out[at, :]
        a = m * g
        b = m * pltpu.roll(g, width // 2, 1)
        c_re = a + pltpu.roll(a, width // 2, 1)
        c_im = pltpu.roll(b, width // 2, 1) - b
        out[at, :] = jnp.where(left, c_re, c_im)
        return carry

    lax.fori_loop(0, slots // 8, step, 0, unroll=2)


def sum_kernel(high, low, first, lengths, arrived, c, out, wide):
    total, width = arrived.shape
    slots = c.shape[0]
    group = 256
    span = math.gcd(slots, 512)
    row_block = out.shape[0]
    step_k = math.gcd(total, 1024)
    wide[:, :width] = arrived[...]
    wide[:, width:] = jnp.ones((total, width), jnp.bfloat16)
    out[...] = jnp.zeros(out.shape, jnp.float32)
    left = lax.broadcasted_iota(jnp.int32, (span, width), 1) < width // 2

    def step(t, carry):
        acc = jnp.zeros((span, 2 * width), jnp.float32)
        spots = lax.broadcasted_iota(jnp.int32, (group, step_k), 0).astype(jnp.float32).astype(jnp.bfloat16)
        one = jnp.ones((group, step_k), jnp.bfloat16)
        nil = jnp.zeros((group, step_k), jnp.bfloat16)
        for k in range(total // step_k):
            at = pl.ds(k * step_k, step_k)
            hits = []
            for h in range(span // group):
                mine = jnp.where(high[:, at] == t * (span // group) + h, low[:, at], -1.0)
                mine = jnp.broadcast_to(mine.astype(jnp.bfloat16), (group, step_k))
                hits.append(jnp.where(spots == mine, one, nil))
            acc = acc + jnp.dot(
                jnp.concatenate(hits, axis=0), wide[at, :], preferred_element_type=jnp.float32
            )
        s = acc[:, :width]
        w = acc[:, width:]
        base = pl.multiple_of(t * span, span)
        x = c[pl.ds(base, span), :]
        y = pltpu.roll(x, width // 2, 1)
        c_re = jnp.where(left, x, y)
        c_im = jnp.where(left, y, -x)
        num = c_re * s - c_im * pltpu.roll(s, width // 2, 1)
        den = w * (c_re * c_re + c_im * c_im)
        values = jnp.concatenate([num, den], axis=1)
        ants = lax.broadcasted_iota(jnp.int32, (row_block, span), 0)
        pick = jnp.where(
            ants == first[:, pl.ds(base, span)], lengths[:, pl.ds(base, span)].astype(jnp.float32), 0.0
        ).astype(jnp.bfloat16)
        part = jnp.zeros(out.shape, jnp.float32)
        for _ in range(3):
            piece = values.astype(jnp.bfloat16)
            values = values - piece.astype(jnp.float32)
            part = part + jnp.dot(pick, piece, preferred_element_type=jnp.float32)
        out[...] += part
        return carry

    lax.fori_loop(0, slots // span, step, 0)


def column_gains_of(gains, row_count, col_count, my_row):
    got = []
    for m in range(row_count):
        pairs = []
        for col in range(col_count):
            for row in range(row_count):
                pairs.append((col * row_count + (m + row) % row_count, row * col_count + col))
        got.append(lax.ppermute(gains, ("arow", "acol"), pairs))
    stacked = jnp.concatenate(got + got, axis=0)
    height = gains.shape[0]
    start = (row_count - my_row) % row_count * height
    return lax.dynamic_slice_in_dim(stacked, start, row_count * height, 0)


def local(row_data, row_baseline, pair_table, lengths, model_vis, gains):
    row_count = lax.axis_size("arow")
    col_count = lax.axis_size("acol")
    devices = row_count * col_count
    count_rows, width = row_data.shape
    slots = lengths.shape[0]
    capacity = 4 * count_rows // devices
    total = devices * capacity
    row_block, col_block = model_vis.shape[:2]
    my_row = lax.axis_index("arow")
    my_col = lax.axis_index("acol")
    column_gains = column_gains_of(gains, row_count, col_count, my_row)

    owner = row_baseline // slots
    local_id = row_baseline - owner * slots
    hits = (owner[:, None] == jnp.arange(devices, dtype=jnp.int32)[None, :]).astype(jnp.bfloat16)
    step_rows = math.gcd(count_rows, 128)
    blocks = hits.reshape(count_rows // step_rows, step_rows, devices)
    positions = jnp.arange(step_rows, dtype=jnp.int32)
    lower = (positions[:, None] > positions[None, :]).astype(jnp.bfloat16)
    within = jnp.einsum("ij,bjd->bid", lower, blocks, preferred_element_type=jnp.float32)
    per_block = jnp.sum(blocks, axis=1, dtype=jnp.float32)
    before = jnp.cumsum(per_block, axis=0) - per_block
    ranking = jnp.sum(
        (within + before[:, None, :]) * blocks.astype(jnp.float32), axis=2
    ).reshape(count_rows)
    counts = jnp.sum(per_block, axis=0).astype(jnp.int32)
    target = owner * capacity + ranking.astype(jnp.int32)

    smem = pl.BlockSpec(memory_space=pltpu.SMEM)
    vmem = pl.BlockSpec(memory_space=pltpu.VMEM)
    outgoing, tags = pl.pallas_call(
        pack_kernel,
        in_specs=[smem, smem, vmem],
        out_specs=[vmem, smem],
        out_shape=[
            jax.ShapeDtypeStruct((total, width), jnp.bfloat16),
            jax.ShapeDtypeStruct((total,), jnp.int32),
        ],
        scratch_shapes=[
            pltpu.VMEM((count_rows, width), jnp.float32),
            pltpu.VMEM((total, width), jnp.float32),
        ],
        compiler_params=pltpu.CompilerParams(vmem_limit_bytes=BIG),
        name="pack",
    )(target, local_id, row_data)
    labels = jnp.where(
        jnp.arange(capacity, dtype=jnp.int32)[None, :] < counts[:, None],
        tags.reshape(devices, capacity),
        -1,
    )
    names = lax.all_to_all(labels, ("arow", "acol"), split_axis=0, concat_axis=0, tiled=True)
    arrived = lax.all_to_all(
        outgoing.reshape(devices, capacity, width),
        ("arow", "acol"),
        split_axis=0,
        concat_axis=0,
        tiled=True,
    ).reshape(total, width)

    first = jnp.clip(pair_table[:, 0] - my_row * row_block, 0, row_block - 1)
    second = jnp.clip(pair_table[:, 1] - my_col * col_block, 0, col_block - 1)
    tiles = row_block * col_block // 8
    chunks = math.gcd(tiles, 8)
    c = pl.pallas_call(
        model_kernel,
        in_specs=[smem, smem, vmem, pl.BlockSpec(memory_space=pl.ANY)],
        out_specs=vmem,
        out_shape=jax.ShapeDtypeStruct((slots, width), jnp.float32),
        scratch_shapes=[
            pltpu.VMEM((tiles, 8, width), jnp.bfloat16),
            pltpu.SemaphoreType.DMA((chunks,)),
        ],
        compiler_params=pltpu.CompilerParams(vmem_limit_bytes=BIG),
        name="model",
    )(first * col_block + second, second, column_gains, model_vis.reshape(tiles, 8, width))

    names = names.reshape(1, total)
    high = names >> 8
    low = (names & 255).astype(jnp.float32)
    sums = pl.pallas_call(
        sum_kernel,
        in_specs=[vmem] * 6,
        out_specs=vmem,
        out_shape=jax.ShapeDtypeStruct((row_block, 2 * width), jnp.float32),
        scratch_shapes=[pltpu.VMEM((total, 2 * width), jnp.bfloat16)],
        compiler_params=pltpu.CompilerParams(vmem_limit_bytes=BIG),
        name="sums",
    )(high, low, first.reshape(1, slots), lengths.reshape(1, slots), arrived, c)
    share = row_block // col_count
    parts = lax.all_to_all(
        sums.reshape(col_count, share, 2 * width), "acol", split_axis=0, concat_axis=0, tiled=True
    )
    whole = jnp.sum(parts, axis=0)
    return whole[:, :width] / (whole[:, width:] + RIDGE)


def solution(mesh):
    placed = (
        P(("arow", "acol"), None),
        P(("arow", "acol")),
        P(("arow", "acol"), None),
        P(("arow", "acol")),
        P("arow", "acol", None),
        P(("arow", "acol"), None),
    )
    return jax.shard_map(
        local, mesh=mesh, in_specs=placed, out_specs=P(("arow", "acol"), None), check_vma=False
    )
```

time: 536 us -> 184 us (0.34)
  local copies, waits for them, and re-layouts: 341 us -> 2.06 us
  Pallas kernels: 0 us -> 94 us
  matrix products: 69.2 us -> 0.21 us
  blocking collectives: 0 us -> 42.3 us
  waiting for transfers between devices: 60.8 us -> 23.3 us
  other arithmetic: 27 us -> 5.71 us
  between operations: 13.7 us -> 0.13 us
  loops' own time: 10.1 us -> 0 us
    gather x3 -> x0, local copies, waits for them, and re-layouts: 317 us -> none  [the longest x2 290 us: local(): jnp.take(model_vis.reshape(row_block * col_block, width), first * col_blo...]
    pallas_call x0 -> x3, Pallas kernels: none -> 94 us  [the longest x1 53.9 us: local(): pl.pallas_call(model_kernel, in_specs=[smem, smem, vmem, pl.BlockSpec(mem...]
    dot_general x34 -> x0, matrix products: 69 us -> none  [the longest x16 39.3 us: place(): jnp.dot(table, row_data, preferred_element_type=jnp.float32)]
    psum x1 -> x0, waiting for transfers between devices: 58.4 us -> none  [local(): numer, denom = lax.psum((numer, denom), 'acol')]
    all_to_all x0 -> x2, blocking collectives: none -> 42.3 us  [the longest x1 27.9 us: local(): lax.all_to_all(sums.reshape(col_count, share, 2 * width), 'acol', split_a...]
    ppermute x0 -> x4, waiting for transfers between devices: none -> 23.3 us  [column_gains_of(): got.append(lax.ppermute(gains, ('arow', 'acol'), pairs))]
    select_n x4 -> x1, other arithmetic: 16.3 us -> 0.86 us  [local(): jnp.where(jnp.arange(capacity, dtype=jnp.int32)[None, :] < counts[:, None...]
    ppermute x0 -> x4, starting transfers between devices: none -> 12.4 us  [column_gains_of(): got.append(lax.ppermute(gains, ('arow', 'acol'), pairs))]
  transfers between devices with their start and end apart: 4 -> 5, of which waited for: 2 -> 3; matrix products, arithmetic and copies ran while one was open for 67% -> 1% of each run, Pallas kernels for 0% -> 29%
where the time goes in v1:
time: 184 us; the launch traced here: 183 us
  Pallas kernels  94 us (51%)
  blocking collectives  42.3 us (23%)
  waiting for transfers between devices  23.3 us (13%)
  starting transfers between devices  15.3 us (8%)
  other arithmetic  5.71 us (3%)
  local copies, waits for them, and re-layouts  2.06 us (1%)
    pallas_call x1, Pallas kernels, local(): pl.pallas_call(model_kernel, in_specs=[smem, smem, vmem, pl.BlockSpec(mem...  53.9 us
    pallas_call x1, Pallas kernels, local(): pl.pallas_call(sum_kernel, in_specs=[vmem] * 6, out_specs=vmem, out_shape...  33.3 us
    all_to_all x1, blocking collectives, local(): lax.all_to_all(sums.reshape(col_count, share, 2 * width), 'acol', split_a...  27.9 us
    ppermute x4, waiting for transfers between devices, column_gains_of(): got.append(lax.ppermute(gains, ('arow', 'acol'), pairs))  23.3 us
    all_to_all x1, blocking collectives, local(): lax.all_to_all(labels, ('arow', 'acol'), split_axis=0, concat_axis=0, til...  14.4 us
    ppermute x4, starting transfers between devices, column_gains_of(): got.append(lax.ppermute(gains, ('arow', 'acol'), pairs))  12.4 us
    pallas_call x1, Pallas kernels, local(): pl.pallas_call(pack_kernel, in_specs=[smem, smem, vmem], out_specs=[vmem,...  6.79 us
  transfers between devices with their start and end apart: 5, of which 3 were waited for; matrix products, arithmetic and copies ran while one was open for 1% of the time, Pallas kernels for 29%

profile of v1, /device:TPU:0, one launch (start us, length us, event | category | flops | bytes accessed | tf_op | source)
XLA Modules:
  0.0 183.0 jit_solution(9899673497690260963)
XLA Ops:
  0.0 0.7 fusion.10
  0.7 0.2 convert_reduce_fusion.1
  0.9 0.2 fusion.2
  1.2 1.3 multiply_subtract_fusion
  2.5 6.8 %pack.1 = (bf16[8192,128]{1,0:T(8,128)(2,1)}, s32[8192]{0:T(1024)}) custom-call(s32[2048]{0:T(1024)} %get-tuple-element.17.target, s32[2048]{0:T(1024)} %get-tuple-element.16.local_id, bf16[2048,128]{1,0:T(8,128)(2,1)} %rows.1), custom_call_target="tpu_custom_call" | custom-call | tf_op jit(solution)/shard_map/pack/pallas_call | solution.py:174
  9.3 0.9 compare_select_fusion
  10.1 14.4 %all_to_all.16 = s32[32,1,256]{2,1,0:T(1,128)S(1)} all-to-all(s32[32,1,256]{2,1,0:T(1,128)S(1)} %compare_select_fusion), channel_id=1, replica_groups=mesh['arow'=4,'acol'=8] {'arow','acol'}, dimensions={0} | all-to-all | bytes 65536 | tf_op jit(solution)/shard_map/all_to_all | solution.py:194
  24.5 0.0 copy-start.3
  24.5 0.0 copy-start.2
  24.5 2.9 %all-to-all-start.1 = ((bf16[32,256,128]{2,1,0:T(8,128)(2,1)}), bf16[32,256,128]{2,1,0:T(8,128)(2,1)S(1)}, u32[]{:S(2)}, u32[]{:S(2)}) async-start(bf16[32,256,128]{2,1,0:T(8,128)(2,1)} %bitcast.28), calls=%async_computation.1 | async-start | bytes 4194304 | tf_op jit(solution)/shard_map/all_to_all | solution.py:195
  27.4 0.0 copy-done.3
  27.4 0.7 collective-permute-start
  28.1 9.0 %collective-permute-start.1 = (f32[64,128]{1,0:T(8,128)S(1)}, f32[64,128]{1,0:T(8,128)S(1)}, u32[]{:S(2)}, u32[]{:S(2)}) collective-permute-start(f32[64,128]{1,0:T(8,128)S(1)} %copy-done.3), channel_id=1, source_target_pairs={{1,0},{2,8},{3,16},{0,24},{5,1},{6,9},{7,17},{4,25},{9,2},{10,10},... | collective-permute-start | bytes 98312 | tf_op jit(solution)/shard_map/ppermute | solution.py:136
  37.1 0.4 collective-permute-start.2
  37.4 2.4 %collective-permute-start.3 = (f32[64,128]{1,0:T(8,128)S(1)}, f32[64,128]{1,0:T(8,128)S(1)}, u32[]{:S(2)}, u32[]{:S(2)}) collective-permute-start(f32[64,128]{1,0:T(8,128)S(1)} %copy-done.3), channel_id=1, source_target_pairs={{3,0},{0,8},{1,16},{2,24},{7,1},{4,9},{5,17},{6,25},{11,2},{8,10},... | collective-permute-start | bytes 98312 | tf_op jit(solution)/shard_map/ppermute | solution.py:136
  39.9 0.0 copy-done.2
  39.9 0.7 subtract_clamp_fusion
  40.5 0.0 copy-start.1
  40.5 0.6 add.35.key
  41.1 0.0 collective-permute-done
  41.2 22.3 %collective-permute-done.1 = f32[64,128]{1,0:T(8,128)S(1)} collective-permute-done((f32[64,128]{1,0:T(8,128)S(1)}, f32[64,128]{1,0:T(8,128)S(1)}, u32[]{:S(2)}, u32[]{:S(2)}) %collective-permute-start.1) | collective-permute-done | bytes 32800 | tf_op jit(solution)/shard_map/ppermute | solution.py:136
  63.5 0.6 collective-permute-done.2
  64.1 0.3 collective-permute-done.3
  64.5 0.7 constant_dynamic-slice_fusion.gains
  65.2 0.0 copy-done.1
  65.2 53.9 %model.1.c = f32[4096,128]{1,0:T(8,128)} custom-call(s32[4096]{0:T(1024)} %add.35.key, s32[4096]{0:T(1024)} %bitcast.30, f32[256,128]{1,0:T(8,128)} %constant_dynamic-slice_fusion.gains, bf16[16384,8,128]{2,1,0:T(8,128)(2,1)} %bitcast.25), custom_call_target="tpu_custom_call" | custom-call | tf_op jit(solution)/shard_map/model/pallas_call | solution.py:207
  119.1 0.7 and_convert_fusion
  119.7 0.0 all-to-all-done.1
  119.7 0.0 copy-start
  119.7 1.3 copy-done
  121.1 33.3 %sums.1 = f32[512,256]{1,0:T(8,128)} custom-call(s32[1,8192]{1,0:T(1,128)} %bitcast.32, f32[1,8192]{1,0:T(1,128)} %bitcast.31, s32[1,4096]{1,0:T(1,128)} %get-tuple-element.13.first, s32[1,4096]{1,0:T(1,128)} %bitcast.35, bf16[8192,128]{1,0:T(8,128)(2,1)} %bitcast.26, f32[4096,128]{1,0:T(8,128)} %model.1.c), custom_call_target="tpu_custom_call" | custom-call | tf_op jit(solution)/shard_map/sums/pallas_call | solution.py:223
  154.4 27.9 %all_to_all.17 = f32[8,64,256]{2,1,0:T(8,128)S(1)} all-to-all(f32[8,64,256]{2,1,0:T(8,128)} %bitcast.27), channel_id=1, replica_groups=mesh['arow'=4,'acol'=8] {'acol'}, dimensions={0} | all-to-all | bytes 1048576 | tf_op jit(solution)/shard_map/all_to_all | solution.py:233
  182.4 0.6 fusion.7
  (12 shorter events, 0.1 us)
Async XLA Ops:
  24.5 2.9 %copy-start.3 = (f32[64,128]{1,0:T(8,128)S(1)}, f32[64,128]{1,0:T(8,128)}, u32[]{:S(2)}) copy-start(f32[64,128]{1,0:T(8,128)} %param.11) | copy-start | bytes 98308
  24.5 15.3 %copy-start.2 = (s32[4096,2]{0,1:T(2,128)S(1)}, s32[4096,2]{0,1:T(2,128)}, u32[]{:S(2)}) copy-start(s32[4096,2]{0,1:T(2,128)} %param.8) | copy-start | bytes 98308
  24.5 95.2 %all-to-all-start.1 = ((bf16[32,256,128]{2,1,0:T(8,128)(2,1)}), bf16[32,256,128]{2,1,0:T(8,128)(2,1)S(1)}, u32[]{:S(2)}, u32[]{:S(2)}) async-start(bf16[32,256,128]{2,1,0:T(8,128)(2,1)} %bitcast.28), calls=%async_computation.1 | async-start | bytes 4194304 | tf_op jit(solution)/shard_map/all_to_all | solution.py:195
  27.4 13.7 %collective-permute-start = (f32[64,128]{1,0:T(8,128)S(1)}, f32[64,128]{1,0:T(8,128)S(1)}, u32[]{:S(2)}, u32[]{:S(2)}) collective-permute-start(f32[64,128]{1,0:T(8,128)S(1)} %copy-done.3), channel_id=1, source_target_pairs={{0,0},{1,8},{2,16},{3,24},{4,1},{5,9},{6,17},{7,25},{8,2},{9,10},{... | collective-permute-start | bytes 98312 | tf_op jit(solution)/shard_map/ppermute | solution.py:136
  28.1 35.4 %collective-permute-start.1 = (f32[64,128]{1,0:T(8,128)S(1)}, f32[64,128]{1,0:T(8,128)S(1)}, u32[]{:S(2)}, u32[]{:S(2)}) collective-permute-start(f32[64,128]{1,0:T(8,128)S(1)} %copy-done.3), channel_id=1, source_target_pairs={{1,0},{2,8},{3,16},{0,24},{5,1},{6,9},{7,17},{4,25},{9,2},{10,10},... | collective-permute-start | bytes 98312 | tf_op jit(solution)/shard_map/ppermute | solution.py:136
  37.1 27.0 %collective-permute-start.2 = (f32[64,128]{1,0:T(8,128)S(1)}, f32[64,128]{1,0:T(8,128)S(1)}, u32[]{:S(2)}, u32[]{:S(2)}) collective-permute-start(f32[64,128]{1,0:T(8,128)S(1)} %copy-done.3), channel_id=1, source_target_pairs={{2,0},{3,8},{0,16},{1,24},{6,1},{7,9},{4,17},{5,25},{10,2},{11,10}... | collective-permute-start | bytes 98312 | tf_op jit(solution)/shard_map/ppermute | solution.py:136
  37.4 27.0 %collective-permute-start.3 = (f32[64,128]{1,0:T(8,128)S(1)}, f32[64,128]{1,0:T(8,128)S(1)}, u32[]{:S(2)}, u32[]{:S(2)}) collective-permute-start(f32[64,128]{1,0:T(8,128)S(1)} %copy-done.3), channel_id=1, source_target_pairs={{3,0},{0,8},{1,16},{2,24},{7,1},{4,9},{5,17},{6,25},{11,2},{8,10},... | collective-permute-start | bytes 98312 | tf_op jit(solution)/shard_map/ppermute | solution.py:136
  40.5 24.6 %copy-start.1 = (s32[4096,1]{0,1:T(1,128)}, s32[4096,1]{0,1:T(1,128)S(1)}, u32[]{:S(2)}) copy-start(s32[4096,1]{0,1:T(1,128)S(1)} %get-tuple-element.11) | copy-start | bytes 49156
  119.7 1.3 copy-start

commit v2 on v1

--- a/solution.py
+++ b/solution.py
@@ -28,10 +28,10 @@
     out[...] = placed[...].astype(jnp.bfloat16)
 
 
-def model_kernel(key, second, gains, model, out, held, sems):
+def model_kernel(key, model, out, held, sems):
     chunks = sems.shape[0]
     part = held.shape[0] // chunks
-    slots = out.shape[0]
+    slots, width = out.shape
 
     def copy(i):
         return pltpu.make_async_copy(
@@ -40,43 +40,28 @@
 
     for i in range(chunks):
         copy(i).start()
-    width = out.shape[1]
     sub = lax.broadcasted_iota(jnp.int32, (8, width), 0)
-
-    def gain_step(i, carry):
-        acc = jnp.zeros((8, width), jnp.float32)
-        for j in range(8):
-            q = second[i * 8 + j]
-            acc = jnp.where(sub == j, gains[pl.ds(q, 1), :], acc)
-        out[pl.ds(pl.multiple_of(i * 8, 8), 8), :] = acc
-        return carry
-
-    lax.fori_loop(0, slots // 8, gain_step, 0, unroll=2)
     for i in range(chunks):
         copy(i).wait()
-    left = lax.broadcasted_iota(jnp.int32, (8, width), 1) < width // 2
 
     def step(i, carry):
-        m = jnp.zeros((8, width), jnp.float32)
-        for j in range(8):
-            k = key[i * 8 + j]
-            tile = held[k // 8].astype(jnp.float32)
-            m = jnp.where(sub == j, pltpu.roll(tile, (j - k) & 7, 0), m)
-        at = pl.ds(pl.multiple_of(i * 8, 8), 8)
-        g = out[at, :]
-        a = m * g
-        b = m * pltpu.roll(g, width // 2, 1)
-        c_re = a + pltpu.roll(a, width // 2, 1)
-        c_im = pltpu.roll(b, width // 2, 1) - b
-        out[at, :] = jnp.where(left, c_re, c_im)
+        for g in range(4):
+            base = pl.multiple_of(i * 32 + g * 8, 8)
+            m = jnp.zeros((8, width), jnp.float32)
+            for j in range(8):
+                k = key[base + j]
+                tile = held[k >> 3].astype(jnp.float32)
+                m = jnp.where(sub == j, pltpu.roll(tile, (j - k) & 7, 0), m)
+            out[pl.ds(base, 8), :] = m
         return carry
 
-    lax.fori_loop(0, slots // 8, step, 0, unroll=2)
-
-
-def sum_kernel(high, low, first, lengths, arrived, c, out, wide):
+    lax.fori_loop(0, slots // 32, step, 0)
+
+
+def sum_kernel(high, low, first, second, lengths, arrived, model, gains, out, wide, pieces):
     total, width = arrived.shape
-    slots = c.shape[0]
+    slots = model.shape[0]
+    col_block = gains.shape[0]
     group = 256
     span = math.gcd(slots, 512)
     row_block = out.shape[0]
@@ -84,7 +69,11 @@
     wide[:, :width] = arrived[...]
     wide[:, width:] = jnp.ones((total, width), jnp.bfloat16)
     out[...] = jnp.zeros(out.shape, jnp.float32)
-    left = lax.broadcasted_iota(jnp.int32, (span, width), 1) < width // 2
+    rest = gains[...]
+    for i in range(3):
+        piece = rest.astype(jnp.bfloat16)
+        rest = rest - piece.astype(jnp.float32)
+        pieces[:, i * width : (i + 1) * width] = piece
 
     def step(t, carry):
         acc = jnp.zeros((span, 2 * width), jnp.float32)
@@ -104,10 +93,17 @@
         s = acc[:, :width]
         w = acc[:, width:]
         base = pl.multiple_of(t * span, span)
-        x = c[pl.ds(base, span), :]
-        y = pltpu.roll(x, width // 2, 1)
-        c_re = jnp.where(left, x, y)
-        c_im = jnp.where(left, y, -x)
+        cols = lax.broadcasted_iota(jnp.int32, (col_block, span), 0)
+        choose = jnp.where(cols == second[:, pl.ds(base, span)], 1.0, 0.0).astype(jnp.bfloat16)
+        g3 = lax.dot_general(
+            choose, pieces[...], (((0,), (0,)), ((), ())), preferred_element_type=jnp.float32
+        )
+        g = g3[:, :width] + g3[:, width : 2 * width] + g3[:, 2 * width :]
+        m = model[pl.ds(base, span), :]
+        a = m * g
+        b = m * pltpu.roll(g, width // 2, 1)
+        c_re = a + pltpu.roll(a, width // 2, 1)
+        c_im = b - pltpu.roll(b, width // 2, 1)
         num = c_re * s - c_im * pltpu.roll(s, width // 2, 1)
         den = w * (c_re * c_re + c_im * c_im)
         values = jnp.concatenate([num, den], axis=1)
@@ -147,7 +143,9 @@
     count_rows, width = row_data.shape
     slots = lengths.shape[0]
     capacity = 4 * count_rows // devices
-    total = devices * capacity
+    extra = -(-2 * capacity // (16 * width)) * 16
+    stride = capacity + extra
+    total = devices * stride
     row_block, col_block = model_vis.shape[:2]
     my_row = lax.axis_index("arow")
     my_col = lax.axis_index("acol")
@@ -167,7 +165,7 @@
         (within + before[:, None, :]) * blocks.astype(jnp.float32), axis=2
     ).reshape(count_rows)
     counts = jnp.sum(per_block, axis=0).astype(jnp.int32)
-    target = owner * capacity + ranking.astype(jnp.int32)
+    target = owner * stride + ranking.astype(jnp.int32)
 
     smem = pl.BlockSpec(memory_space=pltpu.SMEM)
     vmem = pl.BlockSpec(memory_space=pltpu.VMEM)
@@ -186,27 +184,28 @@
         compiler_params=pltpu.CompilerParams(vmem_limit_bytes=BIG),
         name="pack",
     )(target, local_id, row_data)
-    labels = jnp.where(
-        jnp.arange(capacity, dtype=jnp.int32)[None, :] < counts[:, None],
-        tags.reshape(devices, capacity),
-        -1,
-    )
-    names = lax.all_to_all(labels, ("arow", "acol"), split_axis=0, concat_axis=0, tiled=True)
+    tags = tags.reshape(devices, stride)[:, :capacity]
+    valid = jnp.arange(capacity, dtype=jnp.int32)[None, :] < counts[:, None]
+    marks = jnp.concatenate(
+        [jnp.where(valid, (tags >> 8) + 1, 0), jnp.where(valid, tags & 255, 0)], axis=1
+    ).astype(jnp.bfloat16)
+    marks = jnp.pad(marks, ((0, 0), (0, extra * width - 2 * capacity)))
+    outgoing = lax.dynamic_update_slice(
+        outgoing.reshape(devices, stride, width), marks.reshape(devices, extra, width), (0, capacity, 0)
+    )
     arrived = lax.all_to_all(
-        outgoing.reshape(devices, capacity, width),
-        ("arow", "acol"),
-        split_axis=0,
-        concat_axis=0,
-        tiled=True,
-    ).reshape(total, width)
+        outgoing, ("arow", "acol"), split_axis=0, concat_axis=0, tiled=True
+    )
+    marks = arrived[:, capacity:, :].reshape(devices, extra * width).astype(jnp.float32)
+    arrived = arrived.reshape(total, width)
 
     first = jnp.clip(pair_table[:, 0] - my_row * row_block, 0, row_block - 1)
     second = jnp.clip(pair_table[:, 1] - my_col * col_block, 0, col_block - 1)
     tiles = row_block * col_block // 8
     chunks = math.gcd(tiles, 8)
-    c = pl.pallas_call(
+    model_rows = pl.pallas_call(
         model_kernel,
-        in_specs=[smem, smem, vmem, pl.BlockSpec(memory_space=pl.ANY)],
+        in_specs=[smem, pl.BlockSpec(memory_space=pl.ANY)],
         out_specs=vmem,
         out_shape=jax.ShapeDtypeStruct((slots, width), jnp.float32),
         scratch_shapes=[
@@ -215,20 +214,34 @@
         ],
         compiler_params=pltpu.CompilerParams(vmem_limit_bytes=BIG),
         name="model",
-    )(first * col_block + second, second, column_gains, model_vis.reshape(tiles, 8, width))
-
-    names = names.reshape(1, total)
-    high = names >> 8
-    low = (names & 255).astype(jnp.float32)
+    )(first * col_block + second, model_vis.reshape(tiles, 8, width))
+
+    room = ((0, 0), (0, extra))
+    high = jnp.pad(marks[:, :capacity].astype(jnp.int32) - 1, room, constant_values=-1)
+    low = jnp.pad(marks[:, capacity : 2 * capacity], room)
+    high = high.reshape(1, total)
+    low = low.reshape(1, total)
     sums = pl.pallas_call(
         sum_kernel,
-        in_specs=[vmem] * 6,
+        in_specs=[vmem] * 8,
         out_specs=vmem,
         out_shape=jax.ShapeDtypeStruct((row_block, 2 * width), jnp.float32),
-        scratch_shapes=[pltpu.VMEM((total, 2 * width), jnp.bfloat16)],
+        scratch_shapes=[
+            pltpu.VMEM((total, 2 * width), jnp.bfloat16),
+            pltpu.VMEM((col_block, 3 * width), jnp.bfloat16),
+        ],
         compiler_params=pltpu.CompilerParams(vmem_limit_bytes=BIG),
         name="sums",
-    )(high, low, first.reshape(1, slots), lengths.reshape(1, slots), arrived, c)
+    )(
+        high,
+        low,
+        first.reshape(1, slots),
+        second.reshape(1, slots),
+        lengths.reshape(1, slots),
+        arrived,
+        model_rows,
+        column_gains,
+    )
     share = row_block // col_count
     parts = lax.all_to_all(
         sums.reshape(col_count, share, 2 * width), "acol", split_axis=0, concat_axis=0, tiled=True

time: 184 us -> 126 us (0.68)
  Pallas kernels: 94 us -> 65 us
  blocking collectives: 42.3 us -> 15.1 us
  waiting for transfers between devices: 23.3 us -> 17.2 us
  starting transfers between devices: 15.3 us -> 19.9 us
  local copies, waits for them, and re-layouts: 2.06 us -> 4.04 us
    pallas_call x2, Pallas kernels: 87.2 us -> 58.1 us  [the longest x1 35.8 us: local(): pl.pallas_call(sum_kernel, in_specs=[vmem] * 8, out_specs=vmem, out_shape...]
    ppermute x4, waiting for transfers between devices: 23.3 us -> 3.58 us  [column_gains_of(): got.append(lax.ppermute(gains, ('arow', 'acol'), pairs))]
    all_to_all x1 -> x0, blocking collectives: 14.4 us -> none  [local(): lax.all_to_all(labels, ('arow', 'acol'), split_axis=0, concat_axis=0, til...]
    all_to_all x1, waiting for transfers between devices: 0.01 us -> 13.6 us  [local(): lax.all_to_all(outgoing, ('arow', 'acol'), split_axis=0, concat_axis=0, t...]
    all_to_all x1, blocking collectives: 27.9 us -> 15.1 us  [local(): lax.all_to_all(sums.reshape(col_count, share, 2 * width), 'acol', split_a...]
    all_to_all x1, starting transfers between devices: 2.86 us -> 7.33 us  [local(): lax.all_to_all(outgoing, ('arow', 'acol'), split_axis=0, concat_axis=0, t...]
    reshape x0 -> x3, local copies, waits for them, and re-layouts: none -> 2.53 us  [the longest x1 0.95 us: local(): high = high.reshape(1, total)]
  transfers between devices with their start and end apart: 5 -> 5, of which waited for: 3 -> 4; matrix products, arithmetic and copies ran while one was open for 1% -> 1% of each run, Pallas kernels for 29% -> 18%
where the time goes in v2:
time: 126 us
  Pallas kernels  65 us (52%)
  starting transfers between devices  19.9 us (16%)
  waiting for transfers between devices  17.2 us (14%)
  blocking collectives  15.1 us (12%)
  other arithmetic  4.29 us (3%)
  local copies, waits for them, and re-layouts  4.04 us (3%)
    pallas_call x1, Pallas kernels, local(): pl.pallas_call(sum_kernel, in_specs=[vmem] * 8, out_specs=vmem, out_shape...  35.8 us
    pallas_call x1, Pallas kernels, local(): pl.pallas_call(model_kernel, in_specs=[smem, pl.BlockSpec(memory_space=pl...  22.4 us
    all_to_all x1, blocking collectives, local(): lax.all_to_all(sums.reshape(col_count, share, 2 * width), 'acol', split_a...  15.1 us
    all_to_all x1, waiting for transfers between devices, local(): lax.all_to_all(outgoing, ('arow', 'acol'), split_axis=0, concat_axis=0, t...  13.6 us
    ppermute x4, starting transfers between devices, column_gains_of(): got.append(lax.ppermute(gains, ('arow', 'acol'), pairs))  12.5 us
    all_to_all x1, starting transfers between devices, local(): lax.all_to_all(outgoing, ('arow', 'acol'), split_axis=0, concat_axis=0, t...  7.33 us
    pallas_call x1, Pallas kernels, local(): pl.pallas_call(pack_kernel, in_specs=[smem, smem, vmem], out_specs=[vmem,...  6.86 us
    ppermute x4, waiting for transfers between devices, column_gains_of(): got.append(lax.ppermute(gains, ('arow', 'acol'), pairs))  3.58 us
  transfers between devices with their start and end apart: 5, of which 4 were waited for; matrix products, arithmetic and copies ran while one was open for 1% of the time, Pallas kernels for 18%

profile of v2, /device:TPU:0, one launch (start us, length us, event | category | flops | bytes accessed | tf_op | source)
XLA Modules:
  0.0 125.9 jit_solution(3176683963220139636)
XLA Ops:
  0.0 1.3 %multiply_subtract_fusion = (s32[2048]{0:T(1024)}, s32[16,128]{1,0:T(8,128)S(1)}) fusion(s32[2048]{0:T(1024)} %param.7), kind=kLoop, calls=%fused_computation.42 | loop fusion | flops 34816 | bytes 24576 | tf_op jit(solution)/shard_map/sub | solution.py:155
  1.3 0.2 convert_reduce_fusion
  1.5 0.2 fusion.2
  1.8 1.3 %bitcast_add_fusion.target = s32[2048]{0:T(1024)} fusion(f32[16,128]{1,0:T(8,128)S(1)} %fusion.2, s32[2048]{0:T(1024)} %param.7), kind=kLoop, calls=%fused_computation.41 | loop fusion | flops 36864 | bytes 24576 | tf_op jit(solution)/shard_map/add | solution.py:168
  3.1 6.9 %pack.1 = (bf16[8704,128]{1,0:T(8,128)(2,1)}, s32[8704]{0:T(1024)}) custom-call(s32[2048]{0:T(1024)} %bitcast_add_fusion.target, s32[2048]{0:T(1024)} %get-tuple-element.16.local_id, bf16[2048,128]{1,0:T(8,128)(2,1)} %rows.1), custom_call_target="tpu_custom_call" | custom-call | tf_op jit(solution)/shard_map/pack/pallas_call | solution.py:172
  9.9 0.9 reshape.113
  10.8 0.1 select_convert_fusion.1
  10.9 0.7 constant_dynamic-update-slice_fusion.8
  11.6 0.0 copy-start.2
  11.6 0.0 copy-start.1
  11.6 7.3 %all-to-all-start = ((bf16[32,272,128]{2,1,0:T(8,128)(2,1)}), bf16[32,272,128]{2,1,0:T(8,128)(2,1)S(1)}, u32[]{:S(2)}, u32[]{:S(2)}) async-start(bf16[32,272,128]{2,1,0:T(8,128)(2,1)} %constant_dynamic-update-slice_fusion.8), calls=%async_computation | async-start | bytes 4456448 | tf_op jit(solution)/shard_map/all_to_all | solution.py:196
  19.0 0.0 copy-done.2
  19.0 0.7 collective-permute-start
  19.6 9.1 %collective-permute-start.1 = (f32[64,128]{1,0:T(8,128)S(1)}, f32[64,128]{1,0:T(8,128)S(1)}, u32[]{:S(2)}, u32[]{:S(2)}) collective-permute-start(f32[64,128]{1,0:T(8,128)S(1)} %copy-done.2), channel_id=1, source_target_pairs={{1,0},{2,8},{3,16},{0,24},{5,1},{6,9},{7,17},{4,25},{9,2},{10,10},... | collective-permute-start | bytes 98312 | tf_op jit(solution)/shard_map/ppermute | solution.py:132
  28.7 0.3 collective-permute-start.2
  29.1 2.5 %collective-permute-start.3 = (f32[64,128]{1,0:T(8,128)S(1)}, f32[64,128]{1,0:T(8,128)S(1)}, u32[]{:S(2)}, u32[]{:S(2)}) collective-permute-start(f32[64,128]{1,0:T(8,128)S(1)} %copy-done.2), channel_id=1, source_target_pairs={{3,0},{0,8},{1,16},{2,24},{7,1},{4,9},{5,17},{6,25},{11,2},{8,10},... | collective-permute-start | bytes 98312 | tf_op jit(solution)/shard_map/ppermute | solution.py:132
  31.5 0.0 copy-done.1
  31.6 0.7 multiply_add_fusion
  32.2 22.4 %model.1 = f32[4096,128]{1,0:T(8,128)} custom-call(s32[4096]{0:T(1024)} %bitcast.38, bf16[16384,8,128]{2,1,0:T(8,128)(2,1)} %bitcast.30), custom_call_target="tpu_custom_call" | custom-call | tf_op jit(solution)/shard_map/model/pallas_call | solution.py:206
  54.6 0.0 collective-permute-done
  54.6 2.5 %collective-permute-done.1 = f32[64,128]{1,0:T(8,128)S(1)} collective-permute-done((f32[64,128]{1,0:T(8,128)S(1)}, f32[64,128]{1,0:T(8,128)S(1)}, u32[]{:S(2)}, u32[]{:S(2)}) %collective-permute-start.1) | collective-permute-done | bytes 32800 | tf_op jit(solution)/shard_map/ppermute | solution.py:132
  57.1 0.7 collective-permute-done.2
  57.8 0.4 collective-permute-done.3
  58.2 0.7 constant_dynamic-slice_fusion.gains
  58.9 13.6 %all-to-all-done = bf16[32,272,128]{2,1,0:T(8,128)(2,1)S(1)} async-done(((bf16[32,272,128]{2,1,0:T(8,128)(2,1)}), bf16[32,272,128]{2,1,0:T(8,128)(2,1)S(1)}, u32[]{:S(2)}, u32[]{:S(2)}) %all-to-all-start) | async-done | bytes 2228256 | tf_op jit(solution)/shard_map/all_to_all | solution.py:196
  72.5 0.0 copy-start
  72.5 0.1 copy.10
  72.6 0.9 reshape.115.high
  73.6 0.7 reshape.116.low
  74.3 0.0 copy-done
  74.3 35.8 %sums.1 = f32[512,256]{1,0:T(8,128)} custom-call(s32[1,8704]{1,0:T(1,128)} %reshape.115.high, f32[1,8704]{1,0:T(1,128)} %reshape.116.low, s32[1,4096]{1,0:T(1,128)} %get-tuple-element.15.first, s32[1,4096]{1,0:T(1,128)} %get-tuple-element.14.second, s32[1,4096]{1,0:T(1,128)} %bitcast.39, bf16[8704,128]{1,0:T(8,128)(2,1)} %bitcast.31, f32[4096,128]{1,0:T(8,128)} %model.1, ...), custom_call_target="tpu_custom_call" | custom-call | tf_op jit(solution)/shard_map/sums/pallas_call | solution.py:224
  110.1 15.1 %all_to_all.10 = f32[8,64,256]{2,1,0:T(8,128)S(1)} all-to-all(f32[8,64,256]{2,1,0:T(8,128)} %bitcast.33), channel_id=1, replica_groups=mesh['arow'=4,'acol'=8] {'acol'}, dimensions={0} | all-to-all | bytes 1048576 | tf_op jit(solution)/shard_map/all_to_all | solution.py:246
  125.2 0.6 fusion.11
  (19 shorter events, 0.2 us)
Async XLA Ops:
  11.6 7.3 %copy-start.2 = (f32[64,128]{1,0:T(8,128)S(1)}, f32[64,128]{1,0:T(8,128)}, u32[]{:S(2)}) copy-start(f32[64,128]{1,0:T(8,128)} %param.11) | copy-start | bytes 98308
  11.6 19.9 %copy-start.1 = (s32[4096,2]{0,1:T(2,128)S(1)}, s32[4096,2]{0,1:T(2,128)}, u32[]{:S(2)}) copy-start(s32[4096,2]{0,1:T(2,128)} %param.8) | copy-start | bytes 98308
  11.6 60.9 %all-to-all-start = ((bf16[32,272,128]{2,1,0:T(8,128)(2,1)}), bf16[32,272,128]{2,1,0:T(8,128)(2,1)S(1)}, u32[]{:S(2)}, u32[]{:S(2)}) async-start(bf16[32,272,128]{2,1,0:T(8,128)(2,1)} %constant_dynamic-update-slice_fusion.8), calls=%async_computation | async-start | bytes 4456448 | tf_op jit(solution)/shard_map/all_to_all | solution.py:196
  19.0 35.6 %collective-permute-start = (f32[64,128]{1,0:T(8,128)S(1)}, f32[64,128]{1,0:T(8,128)S(1)}, u32[]{:S(2)}, u32[]{:S(2)}) collective-permute-start(f32[64,128]{1,0:T(8,128)S(1)} %copy-done.2), channel_id=1, source_target_pairs={{0,0},{1,8},{2,16},{3,24},{4,1},{5,9},{6,17},{7,25},{8,2},{9,10},{... | collective-permute-start | bytes 98312 | tf_op jit(solution)/shard_map/ppermute | solution.py:132
  19.6 37.5 %collective-permute-start.1 = (f32[64,128]{1,0:T(8,128)S(1)}, f32[64,128]{1,0:T(8,128)S(1)}, u32[]{:S(2)}, u32[]{:S(2)}) collective-permute-start(f32[64,128]{1,0:T(8,128)S(1)} %copy-done.2), channel_id=1, source_target_pairs={{1,0},{2,8},{3,16},{0,24},{5,1},{6,9},{7,17},{4,25},{9,2},{10,10},... | collective-permute-start | bytes 98312 | tf_op jit(solution)/shard_map/ppermute | solution.py:132
  28.7 29.1 %collective-permute-start.2 = (f32[64,128]{1,0:T(8,128)S(1)}, f32[64,128]{1,0:T(8,128)S(1)}, u32[]{:S(2)}, u32[]{:S(2)}) collective-permute-start(f32[64,128]{1,0:T(8,128)S(1)} %copy-done.2), channel_id=1, source_target_pairs={{2,0},{3,8},{0,16},{1,24},{6,1},{7,9},{4,17},{5,25},{10,2},{11,10}... | collective-permute-start | bytes 98312 | tf_op jit(solution)/shard_map/ppermute | solution.py:132
  29.1 29.1 %collective-permute-start.3 = (f32[64,128]{1,0:T(8,128)S(1)}, f32[64,128]{1,0:T(8,128)S(1)}, u32[]{:S(2)}, u32[]{:S(2)}) collective-permute-start(f32[64,128]{1,0:T(8,128)S(1)} %copy-done.2), channel_id=1, source_target_pairs={{3,0},{0,8},{1,16},{2,24},{7,1},{4,9},{5,17},{6,25},{11,2},{8,10},... | collective-permute-start | bytes 98312 | tf_op jit(solution)/shard_map/ppermute | solution.py:132
  72.5 1.8 %copy-start = (bf16[32,272,128]{2,1,0:T(8,128)(2,1)}, bf16[32,272,128]{2,1,0:T(8,128)(2,1)S(1)}, u32[]{:S(2)}) copy-start(bf16[32,272,128]{2,1,0:T(8,128)(2,1)S(1)} %all-to-all-done) | copy-start | bytes 6684676
